TPU v7x, 32 devices: a whole 2x2x4 slice. The times are simulated.
32 devices in a mesh: lat: 16 (over z, x, core), chan: 2 (over y).
Axes of the slice: x: 2, y: 2, z: 4, core: 2. Of those that a mesh axis runs over, the one named last changes fastest.
Arguments:
- ocean_state: bfloat16 [384, 256, 1440], P('lat', 'chan'), may hold values from -6 to 6
- land_mask: int32 [384, 1440], P('lat', 'chan'), may hold values 0 or 1
- order_table: int32 [384], replicated, may hold values from 0 to 383, each once
- spectral_weight: bfloat16 [384, 2, 256, 256], P('lat', None, 'chan'), may hold values from -0.25 to 0.25
- inner_weight: bfloat16 [256, 512], P(None, 'chan'), may hold values from -0.375 to 0.375
- outer_weight: bfloat16 [512, 256], P('chan'), may hold values from -0.25 to 0.25
Outputs:
- layer_output: bfloat16 [384, 1440, 256], P('lat', 'chan')
Inputs may be any that keep to these rules, and one draw needn't show every extreme that they name: `order_table`: a permutation: every order from 0 to 383 stands in exactly one slot.
All inputs are finite; a program needn't handle non-finite values. Where the computation divides by a largest or mean magnitude, that divisor is 1e-20 or more. No bound on the sum of `land_mask` on one device may be relied on, other than what follows from the above.
Results may differ from a plain program's by a relative error of at most 0.0095.
Values may be sent and summed in bfloat16 or wider, within the bound.
No kernel may reach another device: no remote copies, remote signals or barrier semaphores. Data moves between devices by JAX's collectives and lax.ppermute only.
A program may use at most 128 MiB of HBM per device.

v0:
```python
import math

import jax
import jax.numpy as jnp
from jax import lax
from jax.sharding import PartitionSpec as P

NLAT = 384
NLON = 1440
MODES = 384


def fejer_weights():
    colatitude = (jnp.arange(NLAT, dtype=jnp.float32) + 0.5) * (math.pi / NLAT)
    harmonic = jnp.arange(1, NLAT // 2 + 1).astype(jnp.float32)
    series = (
        jnp.cos(2.0 * colatitude[:, None] * harmonic[None, :])
        / (4.0 * harmonic * harmonic - 1.0)[None, :]
    )
    return 2.0 / NLAT * (1.0 - 2.0 * jnp.sum(series, axis=1))


def compose(earlier, latter):
    first_mat, first_log = earlier
    second_mat, second_log = latter
    product = jnp.stack(
        [
            second_mat[0] * first_mat[0] + second_mat[1] * first_mat[2],
            second_mat[0] * first_mat[1] + second_mat[1] * first_mat[3],
            second_mat[2] * first_mat[0] + second_mat[3] * first_mat[2],
            second_mat[2] * first_mat[1] + second_mat[3] * first_mat[3],
        ]
    )
    largest = jnp.max(jnp.abs(product), axis=0, keepdims=True)
    return (product / largest, first_log + second_log + jnp.log(largest))


def legendre_rows(order_value):
    half_rows = NLAT // 2
    colatitude = (jnp.arange(half_rows, dtype=jnp.float32) + 0.5) * (math.pi / NLAT)
    cosine = jnp.cos(colatitude)
    sine_part = jnp.sin(colatitude)
    offsets = jnp.arange(MODES).astype(jnp.float32)
    order_float = order_value.astype(jnp.float32)
    degree = order_float + offsets
    beyond_start = offsets >= 1.0
    denominator = jnp.where(beyond_start, degree * degree - order_float * order_float, 1.0)
    upper_coef = jnp.sqrt((4.0 * degree * degree - 1.0) / denominator)
    previous = degree - 1.0
    lower_coef = jnp.sqrt(
        jnp.maximum(previous * previous - order_float * order_float, 0.0)
        / jnp.maximum(4.0 * previous * previous - 1.0, 1.0)
    )
    filled = jnp.ones((MODES, half_rows), jnp.float32)
    beyond_column = beyond_start[:, None]
    matrix = jnp.stack(
        [
            jnp.where(beyond_column, upper_coef[:, None] * cosine[None, :], filled),
            jnp.where(beyond_column, -(upper_coef * lower_coef)[:, None] * filled, 0.0 * filled),
            jnp.where(beyond_column, filled, 0.0 * filled),
            jnp.where(beyond_column, 0.0 * filled, filled),
        ]
    )
    log_scale = jnp.zeros((1, MODES, half_rows), jnp.float32)
    matrix, log_scale = lax.associative_scan(compose, (matrix, log_scale), axis=1)
    steps_log = 0.5 * jnp.log((2.0 * offsets + 3.0) / (2.0 * offsets + 2.0))
    cumulative = jnp.cumsum(steps_log) - steps_log
    picked = jnp.sum(jnp.where(jnp.arange(MODES) == order_value, cumulative, 0.0 * cumulative))
    start_log = 0.5 * math.log(0.5) + picked + order_float * jnp.log(sine_part)
    northern = jnp.exp(start_log[None, :] + log_scale[0]) * matrix[0]
    northern = jnp.where((offsets < MODES - order_float)[:, None], northern, 0.0 * filled)
    parity = jnp.where(jnp.arange(MODES) % 2 == 0, 1.0, -1.0).astype(jnp.float32)
    return jnp.concatenate([northern, northern[:, ::-1] * parity[:, None]], axis=1)


def fourier_tables(orders):
    longitude = jnp.arange(NLON)
    phase_index = orders[:, None] * longitude[None, :] % NLON
    angles = phase_index.astype(jnp.float32) * (2.0 * math.pi / NLON)
    cosine = jnp.cos(angles)
    sine_part = jnp.sin(angles)
    forward = (
        jnp.concatenate([cosine, -sine_part], axis=0) * (math.sqrt(2.0 * math.pi) / NLON)
    ).astype(jnp.bfloat16)
    factor = jnp.where(orders == 0, 1.0, 2.0).astype(jnp.float32) / math.sqrt(2.0 * math.pi)
    inverse = jnp.concatenate(
        [cosine * factor[:, None], -sine_part * factor[:, None]], axis=0
    ).astype(jnp.bfloat16)
    return (forward, inverse)


def mixing_blocks(weights):
    real_part = weights[:, 0]
    imag_part = weights[:, 1]
    return jnp.stack(
        [jnp.stack([real_part, imag_part], axis=1), jnp.stack([-imag_part, real_part], axis=1)],
        axis=1,
    )


def local(ocean_state, land_mask, order_table, spectral_weight, inner_weight, outer_weight):
    local_rows = ocean_state.shape[0]
    local_channels = ocean_state.shape[1]
    slots_here = spectral_weight.shape[0]
    forward, inverse = fourier_tables(order_table)
    flat_state = ocean_state.reshape(local_rows * local_channels, NLON)
    coeffs = lax.dot_general(
        flat_state, forward, (((1,), (1,)), ((), ())), preferred_element_type=jnp.float32
    )
    coeffs = coeffs.astype(jnp.bfloat16).reshape(local_rows, local_channels, 2, MODES)
    owned_coeffs = lax.all_to_all(coeffs, "lat", split_axis=3, concat_axis=0, tiled=True)
    first_slot = lax.axis_index("lat") * slots_here
    my_orders = lax.dynamic_slice_in_dim(order_table, first_slot, slots_here)
    tables = lax.map(legendre_rows, my_orders)
    weighted = (tables * fejer_weights()[None, None, :]).astype(jnp.bfloat16)
    plain_table = tables.astype(jnp.bfloat16)
    spectra = jnp.einsum(
        "rcpm,mkr->mpck", owned_coeffs, weighted, preferred_element_type=jnp.float32
    ).astype(jnp.bfloat16)
    gathered = lax.all_gather(spectra, "chan", axis=2, tiled=True)
    blocks = mixing_blocks(spectral_weight)
    mixed_spec = jnp.einsum(
        "mpck,mpqdc->mqdk", gathered, blocks, preferred_element_type=jnp.float32
    ).astype(jnp.bfloat16)
    synthesis = jnp.einsum(
        "mqdk,mkr->rdqm", mixed_spec, plain_table, preferred_element_type=jnp.float32
    ).astype(jnp.bfloat16)
    rows_back = lax.all_to_all(synthesis, "lat", split_axis=0, concat_axis=3, tiled=True)
    spatial = jnp.dot(
        rows_back.reshape(local_rows * local_channels, 2 * MODES),
        inverse,
        preferred_element_type=jnp.float32,
    )
    spatial = spatial.reshape(local_rows, local_channels, NLON)
    hidden = (ocean_state.astype(jnp.float32) + spatial).astype(jnp.bfloat16)
    points = lax.all_to_all(hidden, "chan", split_axis=2, concat_axis=1, tiled=True)
    inner_full, outer_full = (
        lax.all_gather(inner_weight, "chan", axis=1, tiled=True),
        lax.all_gather(outer_weight, "chan", axis=0, tiled=True),
    )
    pre_act = jnp.einsum("rcp,ch->rph", points, inner_full, preferred_element_type=jnp.float32)
    activated = jax.nn.gelu(pre_act).astype(jnp.bfloat16)
    update = jnp.einsum("rph,hc->rpc", activated, outer_full, preferred_element_type=jnp.float32)
    ocean_mask = land_mask.astype(jnp.float32)
    residual_part = jnp.transpose(points, (0, 2, 1)).astype(jnp.float32)
    return (ocean_mask[:, :, None] * (residual_part + update)).astype(jnp.bfloat16)


def solution(mesh):
    placed = (
        P("lat", "chan", None),
        P("lat", "chan"),
        P(),
        P("lat", None, "chan", None),
        P(None, "chan"),
        P("chan", None),
    )
    return jax.shard_map(
        local, mesh=mesh, in_specs=placed, out_specs=P("lat", "chan", None), check_vma=False
    )
```

profile of v0, /device:TPU:0, one launch (start us, length us, event | category | flops | bytes accessed | tf_op | source)
XLA Modules:
  0.0 1468.0 jit_solution(10121995507402593260)
XLA Ops:
  7.2 11.2 multiply_convert_fusion.2
  18.4 10.3 fusion.83
  28.7 3.6 copy.80
  32.3 11.8 copy.57
  44.1 7.4 all-to-all-start
  53.0 933.0 %while.13 = (s32[]{:T(128)}, f32[24,384,384]{2,1,0:T(8,128)}, s32[24]{0:T(128)}, s32[]{:T(128)}, f32[]{:T(128)}, /*index=5*/f32[]{:T(128)}, f32[]{:T(128)}) while((s32[]{:T(128)}, f32[24,384,384]{2,1,0:T(8,128)}, s32[24]{0:T(128)}, s32[]{:T(128)}, f32[]{:T(128)}, /*index=5*/f32[]{:T(128)}, f32[]{:T(128)}) %tuple.122), condition=%wide.region_20.21_spmd, body=%wide.region_0.20_spmd.sunk | while | flops 9975949 | bytes 54367292 | solution.py:114
  73.3 2.9 pad.1097
  112.1 2.9 pad.1097
  151.0 2.9 pad.1097
  189.8 2.9 pad.1097
  228.7 2.9 pad.1097
  267.5 2.9 pad.1097
  306.4 2.9 pad.1097
  345.2 2.9 pad.1097
  384.0 2.9 pad.1097
  422.9 2.9 pad.1097
  461.8 2.9 pad.1097
  500.6 2.9 pad.1097
  539.4 2.9 pad.1097
  578.3 2.9 pad.1097
  617.1 2.9 pad.1097
  656.0 2.9 pad.1097
  694.9 2.9 pad.1097
  733.8 2.9 pad.1097
  772.6 2.9 pad.1097
  811.4 2.9 pad.1097
  850.3 2.9 pad.1097
  889.1 2.9 pad.1097
  928.0 2.9 pad.1097
  966.8 2.9 pad.1097
  987.1 3.6 copy.58
  990.7 3.4 copy.59
  994.1 11.3 convert_bitcast_fusion.1
  1005.4 1.9 copy-done.10
  1007.5 2.0 maximum_bitcast_fusion.1
  1009.5 115.3 %all-gather.2.cloned.1.call-done = bf16[24,2,256,384]{2,3,1,0:T(8,128)(2,1)} async-done(((bf16[24,2,128,384]{2,3,1,0:T(8,128)(2,1)}), bf16[24,2,256,384]{2,3,1,0:T(8,128)(2,1)}) %all-gather.2.cloned.1.call-update) | async-done | bytes 9437200 | tf_op jit(solution)/shard_map/all_gather | solution.py:120
  1124.9 10.3 fusion.55
  1135.1 11.5 convert_bitcast_fusion
  1146.6 9.4 copy.63
  1156.0 108.9 %all_to_all.51 = bf16[384,128,2,24]{1,2,3,0:T(2,128)(2,1)S(1)} all-to-all(bf16[384,128,2,24]{1,2,3,0:T(2,128)(2,1)} %copy.63), channel_id=1, replica_groups=mesh['lat'=16,'chan'=2] {'lat'}, dimensions={0} | all-to-all | bytes 9437184 | tf_op jit(solution)/shard_map/all_to_all | solution.py:128
  1267.1 9.6 add_convert_fusion
  1276.7 16.9 %copy.67 = bf16[24,128,1440]{1,0,2:T(8,128)(2,1)} copy(bf16[24,128,1440]{1,2,0:T(8,128)(2,1)S(1)} %add_convert_fusion) | data formatting | bytes 17694720 | tf_op jit(solution)/shard_map/convert_element_type | solution.py:135
  1293.6 7.2 all-to-all-start.2
  1300.9 101.3 %all_gather.10 = bf16[256,512]{1,0:T(8,128)(2,1)S(1)} all-gather(bf16[256,256]{1,0:T(8,128)(2,1)S(1)} %copy-done.19), channel_id=1, replica_groups=mesh['lat'=16,'chan'=2] {'chan'}, dimensions={1}, use_global_device_ids=true | all-gather | bytes 393216 | tf_op jit(solution)/shard_map/all_gather | solution.py:138
  1402.2 6.2 all_gather.11
  1408.4 14.3 copy.102
  1422.7 20.0 %all_to_all.47 = bf16[24,256,720]{1,2,0:T(8,128)(2,1)} reshape(bf16[24,2,128,720]{2,1,3,0:T(2,128)(2,1)} %bitcast.169) | data formatting | bytes 17694720 | tf_op jit(solution)/shard_map/all_to_all | solution.py:136
  1442.7 18.0 %fusion.52 = bf16[24,720,256]{2,1,0:T(8,128)(2,1)} fusion(bf16[24,256,720]{1,2,0:T(8,128)(2,1)} %all_to_all.47, f32[24,720]{1,0:T(8,128)S(1)} %convert_element_type.124, bf16[512,256]{1,0:T(8,128)(2,1)S(1)} %all_gather.11, bf16[256,512]{1,0:T(8,128)(2,1)S(1)} %all_gather.10), kind=kOutput, calls=%fused_computation.239 | convolution fusion | flops 9157017600 | bytes 18288128 | tf_op jit(solution)/shard_map/rph,hc->rpc/dot_general | solution.py:143
  (5763 shorter events, 810.7 us)
Async XLA Ops:
  44.1 943.0 %all-to-all-start = ((bf16[24,128,2,384]{1,2,0,3:T(2,128)(2,1)}), bf16[24,128,2,384]{1,2,0,3:T(2,128)(2,1)}, u32[]{:S(2)}, u32[]{:S(2)}) async-start(bf16[24,128,2,384]{1,2,0,3:T(2,128)(2,1)} %copy.57), calls=%async_computation | async-start | bytes 9437184 | tf_op jit(solution)/shard_map/all_to_all | solution.py:111
  51.6 1073.3 %all-gather.2.cloned.1.call-start = ((), (), s32[]{:S(2)}) async-start(), calls=%async_computation.3 | async-start | bytes 14155776 | tf_op jit(solution)/shard_map/all_gather | solution.py:120
  73.2 3.4 copy-start.1
  76.3 10.2 copy-start.4
  112.0 3.4 copy-start.1
  115.1 10.2 copy-start.4
  150.9 3.4 copy-start.1
  153.9 10.2 copy-start.4
  189.7 3.4 copy-start.1
  192.8 10.2 copy-start.4
  228.6 3.4 copy-start.1
  231.7 10.2 copy-start.4
  267.4 3.4 copy-start.1
  270.5 10.2 copy-start.4
  306.3 3.4 copy-start.1
  309.3 10.2 copy-start.4
  345.1 3.4 copy-start.1
  348.2 10.2 copy-start.4
  383.9 3.4 copy-start.1
  387.0 10.2 copy-start.4
  422.8 3.4 copy-start.1
  425.9 10.2 copy-start.4
  461.6 3.4 copy-start.1
  464.7 10.2 copy-start.4
  503.5 10.2 copy-start.4
  539.3 3.4 copy-start.1
  542.4 10.2 copy-start.4
  578.2 3.4 copy-start.1
  581.2 10.2 copy-start.4
  617.0 3.4 copy-start.1
  620.1 10.2 copy-start.4
  659.0 10.2 copy-start.4
  694.8 3.4 copy-start.1
  697.9 10.2 copy-start.4
  736.7 10.2 copy-start.4
  772.5 3.4 copy-start.1
  775.5 10.2 copy-start.4
  814.4 10.2 copy-start.4
  850.1 3.4 copy-start.1
  853.2 10.2 copy-start.4
  889.0 3.4 copy-start.1
  892.1 10.2 copy-start.4
  930.9 10.2 copy-start.4
  969.8 10.2 copy-start.4
  1293.6 7.2 copy-start.21
  1293.6 7.3 copy-start.19
  1293.6 108.6 %copy-start.20 = (bf16[256,256]{1,0:T(8,128)(2,1)S(1)}, bf16[256,256]{1,0:T(8,128)(2,1)}, u32[]{:S(2)}) copy-start(bf16[256,256]{1,0:T(8,128)(2,1)} %param.13) | copy-start | bytes 393220
  1293.6 114.8 %all-to-all-start.2 = ((bf16[24,128,1440]{1,0,2:T(8,128)(2,1)}), bf16[24,128,1440]{1,0,2:T(8,128)(2,1)}, u32[]{:S(2)}, u32[]{:S(2)}) async-start(bf16[24,128,1440]{1,0,2:T(8,128)(2,1)} %copy.67), calls=%async_computation.2 | async-start | bytes 17694720 | tf_op jit(solution)/shard_map/all_to_all | solution.py:136
  (345 other events, 229.6 us)
Sparse Core Ops, SparseCore 0:
  1005.6 119.2 all-gather.1
where the time goes:
time: 1490 us; the launch traced here: 1470 us
  local copies, waits for them, and re-layouts  563 us (38%)
  other arithmetic  414 us (28%)
  blocking collectives  216 us (14%)
  waiting for transfers between devices  115 us (8%)
  matrix products  71 us (5%)
  loops' own time  59.3 us (4%)
    while x840, local copies, waits for them, and re-layouts  257 us
    add x336, other arithmetic, compose(): return (product / largest, first_log + second_log + jnp.log(largest))  183 us
    all_gather x1, waiting for transfers between devices, local(): gathered = lax.all_gather(spectra, 'chan', axis=2, tiled=True)  115 us
    slice x1272, local copies, waits for them, and re-layouts, legendre_rows(): lax.associative_scan(compose, (matrix, log_scale), axis=1)  115 us
    all_to_all x1, blocking collectives, local(): lax.all_to_all(synthesis, 'lat', split_axis=0, concat_axis=3, tiled=True)  109 us
    all_gather x1, blocking collectives, local(): lax.all_gather(inner_weight, 'chan', axis=1, tiled=True)  101 us
    another operation x1, loops' own time, local(): tables = lax.map(legendre_rows, my_orders)  59.3 us
    add x384, other arithmetic, compose(): second_mat[0] * first_mat[0] + second_mat[1] * first_mat[2]  44.1 us

commit v1 on v0

v1 whole, which is shorter than its diff:
```python
import math

import jax
import jax.numpy as jnp
from jax import lax
from jax.experimental import pallas as pl
from jax.experimental.pallas import tpu as pltpu
from jax.sharding import PartitionSpec as P

BF16 = jnp.bfloat16
F32 = jnp.float32
STEP_BITS = 64.0
BIG = 2.0**64
SMALL = 2.0**-64


def fejer_weights(nlat):
    colatitude = (jnp.arange(nlat, dtype=F32) + 0.5) * (math.pi / nlat)
    harmonic = jnp.arange(1, nlat // 2 + 1).astype(F32)
    series = (
        jnp.cos(2.0 * colatitude[:, None] * harmonic[None, :])
        / (4.0 * harmonic * harmonic - 1.0)[None, :]
    )
    return 2.0 / nlat * (1.0 - 2.0 * jnp.sum(series, axis=1))


def legendre_kernel(upper_ref, lower_ref, mant_ref, expo_ref, cos_ref, quad_ref, weighted_ref, *rest):
    plain_refs, rows_ref = rest[:-1], rest[-1]
    width = plain_refs[0].shape[2]
    modes = upper_ref.shape[1]
    nlat = cos_ref.shape[1]
    cosine = jnp.broadcast_to(cos_ref[...], (8, nlat))

    def scales(expo):
        one = jnp.ones_like(expo)
        first = jnp.where(expo < -0.5, one * SMALL, one)
        second = jnp.where(expo < -1.5, one * SMALL, one)
        return first, jnp.where(expo < -2.5, 0.0 * one, second)

    def lane_block(block, carry):
        upper = upper_ref[:, block * 128 : block * 128 + 128]
        lower = lower_ref[:, block * 128 : block * 128 + 128]

        def eight(turn, carry):
            before, last, expo, first, second, upper, lower = carry
            base = pl.multiple_of((block * 128 + turn * 8) * 8, 64)
            for j in range(8):
                a = jnp.broadcast_to(upper[:, j : j + 1], (8, nlat))
                b = jnp.broadcast_to(lower[:, j : j + 1], (8, nlat))
                fresh = (a * cosine) * last - b * before
                before, last = last, fresh
                value = (fresh * first) * second
                for c in range(nlat // 128):
                    rows_ref[c, pl.ds(base + 8 * j, 8), :] = value[:, c * 128 : c * 128 + 128]
            large = jnp.abs(last) > BIG
            before = jnp.where(large, before * SMALL, before)
            last = jnp.where(large, last * SMALL, last)
            expo = jnp.where(large, expo + 1.0, expo)
            first, second = scales(expo)
            upper = pltpu.roll(upper, 120, 1)
            lower = pltpu.roll(lower, 120, 1)
            return before, last, expo, first, second, upper, lower

        out = lax.fori_loop(0, 16, eight, carry + (upper, lower))
        return out[:5]

    expo = expo_ref[...]
    carry = (-mant_ref[...], jnp.zeros((8, nlat), F32), expo) + scales(expo)
    for block in range(modes // 128):
        carry = lane_block(block, carry)
    for c in range(nlat // 128):
        lanes = slice(c * 128, c * 128 + 128)
        quad = quad_ref[:, lanes]
        for k in range(8):
            values = rows_ref[c, pl.ds(k, modes, stride=8), :]
            at = c * 128 % width
            plain_refs[c * 128 // width][k, :, at : at + 128] = values.astype(BF16)
            weighted_ref[k, :, lanes] = (values * quad).astype(BF16)


def row_order(lat, rows, row_step):
    row = jnp.arange(lat * rows, dtype=jnp.int32)
    block, owner, inner = row // (lat * row_step), row // row_step % lat, row % row_step
    return owner * rows + block * row_step + inner


def legendre_tables(orders, row_index, quad, nlat, modes, width):
    slots = orders.shape[0]
    padded = -(-slots // 8) * 8
    orders = jnp.pad(orders, (0, padded - slots))
    half_sign = jnp.where(row_index < nlat // 2, 1.0, -1.0).astype(F32)
    theta = (jnp.minimum(row_index, nlat - 1 - row_index).astype(F32) + 0.5) * (math.pi / nlat)
    cosine = jnp.cos(theta) * half_sign
    order = orders.astype(F32)[:, None]
    offset = jnp.arange(modes).astype(F32)[None, :]
    degree = order + offset
    inside = (offset >= 1.0) & (offset < modes - order)
    upper = jnp.sqrt(
        (4.0 * degree * degree - 1.0)
        / jnp.where(offset >= 1.0, offset * (degree + order), 1.0)
    )
    previous = degree - 1.0
    lower = jnp.sqrt(
        jnp.maximum((offset - 1.0) * (previous + order), 0.0)
        / jnp.maximum(4.0 * previous * previous - 1.0, 1.0)
    )
    upper_coef = jnp.where(inside, upper, 0.0)
    lower_coef = jnp.where(inside, upper * lower, jnp.where(offset < 0.5, 1.0, 0.0))
    steps_log = 0.5 * jnp.log((2.0 * offset + 3.0) / (2.0 * offset + 2.0))
    picked = jnp.sum(jnp.where(offset < order, steps_log, 0.0), axis=1, keepdims=True)
    start_log = 0.5 * math.log(0.5) + picked + order * jnp.log(jnp.sin(theta))[None, :]
    unit = STEP_BITS * math.log(2.0)
    expo = jnp.floor(start_log / unit)
    mant = jnp.exp(start_log - expo * unit)
    eight = lambda wide: pl.BlockSpec((8, wide), lambda g: (g, 0))
    whole = lambda wide: pl.BlockSpec((1, wide), lambda g: (0, 0))
    table = lambda wide: pl.BlockSpec((8, modes, wide), lambda g: (g, 0, 0))
    shape = lambda wide: jax.ShapeDtypeStruct((padded, modes, wide), BF16)
    blocks = nlat // width
    weighted, *plain = pl.pallas_call(
        legendre_kernel,
        grid=(padded // 8,),
        in_specs=[eight(modes), eight(modes), eight(nlat), eight(nlat), whole(nlat), whole(nlat)],
        out_specs=[table(nlat)] + [table(width)] * blocks,
        out_shape=[shape(nlat)] + [shape(width)] * blocks,
        scratch_shapes=[pltpu.VMEM((nlat // 128, modes * 8, 128), F32)],
        cost_estimate=pl.CostEstimate(
            flops=padded * modes * nlat * 16, bytes_accessed=padded * modes * nlat * 4, transcendentals=0
        ),
        name="legendre",
    )(upper_coef, lower_coef, mant, expo, cosine[None, :], quad[None, :])
    return weighted[:slots], [table[:slots] for table in plain]


def fourier_columns(orders, nlon):
    inner = 8 if nlon % 8 == 0 else 1
    slots = orders.shape[0]
    column_order = jnp.repeat(orders, 2)
    part = jnp.tile(jnp.arange(2, dtype=jnp.int32), slots)
    turn = 2.0 * math.pi / nlon

    def pair(steps, shifted):
        phase = (column_order[None, :] * steps[:, None]) % nlon
        angle = phase.astype(F32) * turn
        cosine, sine = jnp.cos(angle), jnp.sin(angle)
        if not shifted:
            return cosine, sine
        odd = (part == 1)[None, :]
        return jnp.where(odd, -sine, cosine), jnp.where(odd, cosine, sine)

    far_cos, far_sin = pair(jnp.arange(nlon // inner, dtype=jnp.int32) * inner, True)
    near_cos, near_sin = pair(jnp.arange(inner, dtype=jnp.int32), False)
    value = far_cos[:, None, :] * near_cos[None] - far_sin[:, None, :] * near_sin[None]
    value = value.reshape(nlon, 2 * slots)
    factor = jnp.where(column_order == 0, 1.0, 2.0).astype(F32) / math.sqrt(2.0 * math.pi)
    forward = (value * (math.sqrt(2.0 * math.pi) / nlon)).astype(BF16)
    inverse = (value * factor[None, :]).astype(BF16)
    return forward, inverse


def mixing_blocks(weights):
    real_part = weights[:, 0]
    imag_part = weights[:, 1]
    return jnp.stack(
        [jnp.stack([real_part, imag_part], axis=1), jnp.stack([-imag_part, real_part], axis=1)],
        axis=1,
    )


def mlp_kernel(chan, here_ref, mask_ref, inner_ref, outer_ref, *rest):
    block_refs, out_ref = rest[:chan], rest[-1]
    channels = block_refs[0].shape[2]
    row = pl.program_id(0)
    lane = lax.broadcasted_iota(jnp.int32, mask_ref.shape, 1)
    mask = jnp.sum(jnp.where(lane == row, mask_ref[...], 0.0), axis=1, keepdims=True)
    points = jnp.concatenate([ref[0] for ref in block_refs], axis=1)
    pre_act = jnp.dot(points, inner_ref[...], preferred_element_type=F32)
    activated = jax.nn.gelu(pre_act).astype(BF16)
    update = jnp.dot(activated, outer_ref[...], preferred_element_type=F32)
    for shift, block_ref in enumerate(block_refs):
        start = pl.multiple_of(lax.rem(here_ref[0] - shift + chan, chan) * channels, channels)
        lanes = slice(shift * channels, (shift + 1) * channels)
        total = mask * (block_ref[0].astype(F32) + update[:, lanes])
        out_ref[0, :, pl.ds(start, channels)] = total.astype(BF16)


def mlp_rows(chan, here, blocks, mask, inner, outer, filled, row, rows, kept_at):
    row_step = mask.shape[0]
    _, piece, channels = blocks[0].shape
    whole = lambda shape: pl.BlockSpec(shape, lambda r, h: (0, 0))
    in_specs = [whole((piece, row_step)), whole(inner.shape), whole(outer.shape)]
    in_specs += [pl.BlockSpec((1, piece, channels), lambda r, h: (r + kept_at, 0, 0))]
    in_specs += [pl.BlockSpec((1, piece, channels), lambda r, h: (r, 0, 0))] * (chan - 1)
    operands = [here.reshape(1), mask.T, inner, outer] + blocks
    aliases = {}
    if filled is not None:
        aliases = {len(operands): 0}
        operands.append(filled)
        in_specs.append(pl.BlockSpec(memory_space=pl.ANY))
    width = chan * channels
    return pl.pallas_call(
        lambda *refs: mlp_kernel(chan, *refs),
        grid_spec=pltpu.PrefetchScalarGridSpec(
            num_scalar_prefetch=1,
            grid=(row_step,),
            in_specs=in_specs,
            out_specs=pl.BlockSpec((1, piece, width), lambda r, h: (r + row, 0, 0)),
        ),
        out_shape=jax.ShapeDtypeStruct((rows, piece, width), BF16),
        input_output_aliases=aliases,
        cost_estimate=pl.CostEstimate(
            flops=4 * row_step * piece * width * inner.shape[1],
            bytes_accessed=4 * row_step * piece * width,
            transcendentals=row_step * piece * inner.shape[1],
        ),
        name="pointwise",
    )(*operands)


def local(lat, chan, ocean_state, land_mask, order_table, spectral_weight, inner_weight, outer_weight):
    rows, channels, nlon = ocean_state.shape
    slots = spectral_weight.shape[0]
    modes = order_table.shape[0]
    nlat = rows * lat
    piece = nlon // chan
    slot_step = 8 if slots % 8 == 0 else slots
    row_step = 8 if rows % 8 == 0 and lat * 8 % 128 == 0 else rows
    width = lat * row_step
    here = lax.axis_index("chan")

    def ring(value, shift):
        return lax.ppermute(value, "chan", [(i, (i + shift) % chan) for i in range(chan)])

    def swap(value):
        return lax.all_to_all(value, "lat", split_axis=0, concat_axis=0, tiled=True)

    inner_full = jnp.concatenate(
        [inner_weight] + [ring(inner_weight, shift) for shift in range(1, chan)], axis=1
    )
    outer_full = jnp.concatenate(
        [outer_weight] + [ring(outer_weight, shift) for shift in range(1, chan)], axis=0
    )
    pieces = [(here + shift) % chan for shift in range(chan)]
    sources = [(here - shift) % chan for shift in range(chan)]
    take = lambda value, at, size, axis: lax.dynamic_slice_in_dim(value, at * size, size, axis=axis)
    ring_inner = jnp.concatenate([take(inner_full, at, channels, 0) for at in sources], axis=0)
    ring_outer = jnp.concatenate([take(outer_full, at, channels, 1) for at in sources], axis=1)
    my_orders = lax.dynamic_slice_in_dim(order_table, lax.axis_index("lat") * slots, slots)
    by_owner = order_table.reshape(lat, slots)
    starts = range(0, slots, slot_step)
    received, inverses = [], []
    for start in starts:
        orders = by_owner[:, start : start + slot_step].reshape(-1)
        forward, inverse = fourier_columns(orders, nlon)
        inverses.append(inverse)
        coeffs = lax.dot_general(
            forward, ocean_state, (((0,), (2,)), ((), ())), preferred_element_type=F32
        ).astype(BF16)
        received.append(swap(coeffs))
    mixers = lax.optimization_barrier(
        [
            [
                mixing_blocks(take(spectral_weight[start : start + slot_step], at, channels, 3))
                for at in sources
            ]
            for start in starts
        ]
    )
    row_index = row_order(lat, rows, row_step)
    quad = fejer_weights(nlat)[row_index]
    mixed, plains = [], []
    for index, (coeffs, start) in enumerate(zip(received, starts)):
        weighted, plain = legendre_tables(
            my_orders[start : start + slot_step], row_index, quad, nlat, modes, width
        )
        plains.append(plain)
        coeffs = coeffs.reshape(lat, slot_step, 2, rows // row_step, row_step, channels)
        coeffs = jnp.transpose(coeffs, (1, 2, 3, 0, 4, 5)).reshape(slot_step, 2, nlat, channels)
        spectra = jnp.einsum(
            "sprc,sir->spic", coeffs, weighted, preferred_element_type=F32
        ).astype(BF16)
        total = None
        for shift in range(chan):
            arrived = spectra if shift == 0 else ring(spectra, shift)
            term = jnp.einsum("spic,spqdc->sqid", arrived, mixers[index][shift], preferred_element_type=F32)
            if shift == 0 and chan > 1:
                term = lax.optimization_barrier(term)
            total = term if total is None else total + term
        mixed.append(total.astype(BF16))
    inverse = jnp.concatenate(inverses, axis=1)
    inverse_of = lax.optimization_barrier(
        [lax.dynamic_slice_in_dim(inverse, at * piece, piece) for at in pieces]
    )
    state = jnp.transpose(ocean_state.reshape(rows, channels, chan, piece), (2, 0, 3, 1))
    state = [
        lax.dynamic_index_in_dim(state, at, 0, keepdims=False) for at in pieces
    ]
    states = lax.optimization_barrier(
        [[value[row : row + row_step] for value in state] for row in range(0, rows, row_step)]
    )
    out, outs = None, []
    count = len(starts)
    for block, row in enumerate(range(0, rows, row_step)):
        back = []
        groups = [list(range(count))]
        if block == 0 and count > 1:
            groups = [list(range(count - 1)), [count - 1]]
        if block == 1 and count > 2:
            groups = [[0], list(range(1, count))]
        for group in groups:
            sent = [
                jnp.einsum("sqid,sir->rsqd", mixed[g], plains[g][block], preferred_element_type=F32)
                .astype(BF16)
                .reshape(lat, row_step, slot_step, 2, channels)
                for g in group
            ]
            sent = jnp.stack(sent, axis=1)
            arrived = swap(sent)
            back.append(jnp.transpose(arrived, (2, 1, 0, 3, 4, 5)).reshape(row_step, -1, channels))
        back = jnp.concatenate(back, axis=1)

        def points(shift):
            spatial = jnp.einsum("rkd,jk->rjd", back, inverse_of[shift], preferred_element_type=F32)
            return (states[block][shift].astype(F32) + spatial).astype(BF16)

        fast = channels % 128 == 0 and piece % 8 == 0
        parts = 2 if fast and row + row_step == rows and row_step % 8 == 0 else 1
        part_rows = row_step // parts
        blocks = [[] for _ in range(parts)]
        for shift in range(1, chan):
            leaving = points(shift)
            for part in range(parts):
                blocks[part].append(ring(leaving[part * part_rows : (part + 1) * part_rows], shift))
        kept = points(0)
        ocean_mask = land_mask[row : row + row_step].astype(F32)
        if fast:
            for part in range(parts):
                at = part * part_rows
                out = mlp_rows(
                    chan,
                    here,
                    [kept] + blocks[part],
                    ocean_mask[at : at + part_rows],
                    ring_inner,
                    ring_outer,
                    out,
                    row + at,
                    rows,
                    at,
                )
            continue
        blocks = [kept] + blocks[0]
        full = jnp.take(jnp.stack(blocks, axis=2), (here - jnp.arange(chan)) % chan, axis=2)
        full = full.reshape(row_step, piece, chan * channels)
        pre_act = jnp.einsum("rpc,ch->rph", full, inner_full, preferred_element_type=F32)
        activated = jax.nn.gelu(pre_act).astype(BF16)
        update = jnp.einsum("rph,hc->rpc", activated, outer_full, preferred_element_type=F32)
        outs.append((ocean_mask[:, :, None] * (full.astype(F32) + update)).astype(BF16))
    return jnp.concatenate(outs, axis=0) if outs else out


def solution(mesh):
    placed = (
        P("lat", "chan", None),
        P("lat", "chan"),
        P(),
        P("lat", None, "chan", None),
        P(None, "chan"),
        P("chan", None),
    )
    lat, chan = mesh.shape["lat"], mesh.shape["chan"]

    def body(*args):
        return local(lat, chan, *args)

    return jax.shard_map(
        body, mesh=mesh, in_specs=placed, out_specs=P("lat", "chan", None), check_vma=False
    )
```

time: 1490 us -> 475 us (0.32)
  local copies, waits for them, and re-layouts: 563 us -> 74.4 us
  other arithmetic: 414 us -> 28.6 us
  blocking collectives: 216 us -> 0 us
  waiting for transfers between devices: 115 us -> 184 us
  loops' own time: 59.3 us -> 0 us
  Pallas kernels: 0 us -> 57.4 us
  starting transfers between devices: 14.7 us -> 66.4 us
  matrix products: 71 us -> 55.9 us
    add x1248 -> x2, other arithmetic: 265 us -> 0.01 us  [legendre_tables(): 0.5 * math.log(0.5) + picked + order * jnp.log(jnp.sin(theta))[None, :]]
    while x840 -> x0, local copies, waits for them, and re-layouts: 257 us -> none
    ppermute x0 -> x9, waiting for transfers between devices: none -> 126 us  [ring(): lax.ppermute(value, 'chan', [(i, (i + shift) % chan) for i in range(chan)])]
    all_gather x1 -> x0, waiting for transfers between devices: 115 us -> none  [local(): gathered = lax.all_gather(spectra, 'chan', axis=2, tiled=True)]
    all_to_all x1 -> x0, blocking collectives: 109 us -> none  [local(): lax.all_to_all(synthesis, 'lat', split_axis=0, concat_axis=3, tiled=True)]
    all_gather x2 -> x0, blocking collectives: 107 us -> none  [the longest x1 101 us: local(): lax.all_gather(inner_weight, 'chan', axis=1, tiled=True)]
    slice x1272 -> x7, local copies, waits for them, and re-layouts: 115 us -> 9.64 us  [the longest x1 6.15 us: local(): value[row:row + row_step]]
    another operation x1 -> x0, loops' own time: 59.3 us -> none  [local(): tables = lax.map(legendre_rows, my_orders)]
where the time goes in v1:
time: 475 us; the launch traced here: 468 us
  waiting for transfers between devices  184 us (39%)
  local copies, waits for them, and re-layouts  74.4 us (16%)
  starting transfers between devices  66.4 us (14%)
  Pallas kernels  57.4 us (12%)
  matrix products  55.9 us (12%)
  other arithmetic  28.6 us (6%)
    ppermute x9, waiting for transfers between devices, ring(): lax.ppermute(value, 'chan', [(i, (i + shift) % chan) for i in range(chan)])  126 us
    all_to_all x8, waiting for transfers between devices, swap(): return lax.all_to_all(value, 'lat', split_axis=0, concat_axis=0, tiled=True)  58.3 us
    all_to_all x8, starting transfers between devices, swap(): return lax.all_to_all(value, 'lat', split_axis=0, concat_axis=0, tiled=True)  56.6 us
    pallas_call x4, Pallas kernels, mlp_rows(): pl.pallas_call(lambda *refs: mlp_kernel(chan, *refs), grid_spec=pltpu.Pre...  31.3 us
    pallas_call x3, Pallas kernels, legendre_tables(): pl.pallas_call(legendre_kernel, grid=(padded // 8,), in_specs=[eight(mode...  26.2 us
    dot_general x3, matrix products, local(): lax.dot_general(forward, ocean_state, (((0,), (2,)), ((), ())), preferred...  16.6 us
    dot_general x6, matrix products, points(): jnp.einsum('rkd,jk->rjd', back, inverse_of[shift], preferred_element_type...  13.5 us
    dot_general x6, matrix products, local(): jnp.einsum('spic,spqdc->sqid', arrived, mixers[index][shift], preferred_e...  13.4 us
  transfers between devices with their start and end apart: 17, of which 11 were waited for; matrix products, arithmetic and copies ran while one was open for 29% of the time, Pallas kernels for 11%

profile of v1, /device:TPU:0, one launch (start us, length us, event | category | flops | bytes accessed | tf_op | source)
XLA Modules:
  0.0 467.8 jit_solution(2990331943033434586)
XLA Ops:
  2.1 2.5 negate_select_fusion.2
  4.6 6.4 %convolution_convert_fusion = bf16[256,24,128]{2,0,1:T(8,128)(2,1)S(1)} fusion(bf16[24,128,1440]{1,2,0:T(8,128)(2,1)} %param.6, f32[8,256]{1,0:T(8,128)S(1)} %get-tuple-element.139, f32[180,256]{1,0:T(8,128)S(1)} %get-tuple-element.132, f32[8,256]{1,0:T(8,128)S(1)} %get-tuple-element.138, f32[180,256]{1,0:T(8,128)S(1)} %get-tuple-element.133), kind=kOutput, calls=%fused_computation.34 | convolution fusion | flops 2267553792 | bytes 10805248 | tf_op jit(solution)/shard_map/dot_general | solution.py:256
  11.1 2.2 copy.155
  13.2 7.7 %all-to-all-start.2 = ((bf16[256,24,128]{2,1,0:T(8,128)(2,1)}), bf16[256,24,128]{2,1,0:T(8,128)(2,1)S(1)}, u32[]{:S(2)}, u32[]{:S(2)}) async-start(bf16[256,24,128]{2,1,0:T(8,128)(2,1)} %copy.155), calls=%async_computation.2 | async-start | bytes 3145728 | tf_op jit(solution)/shard_map/all_to_all | solution.py:235
  24.4 6.3 %convolution_convert_fusion.2 = bf16[256,24,128]{2,0,1:T(8,128)(2,1)S(1)} fusion(bf16[24,128,1440]{1,2,0:T(8,128)(2,1)} %param.6, f32[8,256]{1,0:T(8,128)S(1)} %get-tuple-element.135, f32[180,256]{1,0:T(8,128)S(1)} %get-tuple-element.121, f32[8,256]{1,0:T(8,128)S(1)} %get-tuple-element.134, f32[180,256]{1,0:T(8,128)S(1)} %get-tuple-element.120), kind=kOutput, calls=%fused_computation.36 | convolution fusion | flops 2267553792 | bytes 10805248 | tf_op jit(solution)/shard_map/dot_general | solution.py:256
  30.8 2.2 copy.143
  34.2 3.8 convolution_convert_fusion.1
  38.0 14.7 %all-to-all-done.2 = bf16[256,24,128]{2,1,0:T(8,128)(2,1)S(1)} async-done(((bf16[256,24,128]{2,1,0:T(8,128)(2,1)}), bf16[256,24,128]{2,1,0:T(8,128)(2,1)S(1)}, u32[]{:S(2)}, u32[]{:S(2)}) %all-to-all-start.2) | async-done | bytes 1572896 | tf_op jit(solution)/shard_map/all_to_all | solution.py:235
  53.9 9.1 %all-to-all-start = ((bf16[256,24,128]{2,1,0:T(8,128)(2,1)}), bf16[256,24,128]{2,1,0:T(8,128)(2,1)}, u32[]{:S(2)}, u32[]{:S(2)}) async-start(bf16[256,24,128]{2,1,0:T(8,128)(2,1)} %copy.143), calls=%async_computation | async-start | bytes 3145728 | tf_op jit(solution)/shard_map/all_to_all | solution.py:235
  63.0 2.8 gather_fusion
  66.4 3.7 copy.149
  79.3 15.6 %all-to-all-done = bf16[256,24,128]{2,1,0:T(8,128)(2,1)} async-done(((bf16[256,24,128]{2,1,0:T(8,128)(2,1)}), bf16[256,24,128]{2,1,0:T(8,128)(2,1)}, u32[]{:S(2)}, u32[]{:S(2)}) %all-to-all-start) | async-done | bytes 1572896 | tf_op jit(solution)/shard_map/all_to_all | solution.py:235
  94.9 9.4 %all-to-all-start.1 = ((bf16[256,24,128]{2,1,0:T(8,128)(2,1)}), bf16[256,24,128]{2,1,0:T(8,128)(2,1)}, u32[]{:S(2)}, u32[]{:S(2)}) async-start(bf16[256,24,128]{2,1,0:T(8,128)(2,1)} %copy.149), calls=%async_computation.1 | async-start | bytes 3145728 | tf_op jit(solution)/shard_map/all_to_all | solution.py:235
  106.2 8.7 %legendre.3 = (bf16[8,384,384]{2,1,0:T(8,128)(2,1)}, bf16[8,384,128]{2,1,0:T(8,128)(2,1)}, bf16[8,384,128]{2,1,0:T(8,128)(2,1)}, bf16[8,384,128]{2,1,0:T(8,128)(2,1)}) custom-call(f32[8,384]{1,0:T(8,128)} %get-tuple-element.113.upper_ref, f32[8,384]{1,0:T(8,128)} %get-tuple-element.105.lower_ref, f32[8,384]{1,0:T(8,128)} %get-tuple-element.115.mant_ref, ...), custom_call_target="tpu_custom_call" | custom-call | flops 18874368 | bytes 4718592 | tf_op jit(solution)/shard_map/legendre/pallas_call | solution.py:120
  115.0 8.7 %legendre.4 = (bf16[8,384,384]{2,1,0:T(8,128)(2,1)}, bf16[8,384,128]{2,1,0:T(8,128)(2,1)}, bf16[8,384,128]{2,1,0:T(8,128)(2,1)}, bf16[8,384,128]{2,1,0:T(8,128)(2,1)}) custom-call(f32[8,384]{1,0:T(8,128)} %get-tuple-element.111.upper_ref, f32[8,384]{1,0:T(8,128)} %get-tuple-element.106.lower_ref, f32[8,384]{1,0:T(8,128)} %get-tuple-element.126.mant_ref, ...), custom_call_target="tpu_custom_call" | custom-call | flops 18874368 | bytes 4718592 | tf_op jit(solution)/shard_map/legendre/pallas_call | solution.py:120
  123.7 8.7 %legendre.5 = (bf16[8,384,384]{2,1,0:T(8,128)(2,1)}, bf16[8,384,128]{2,1,0:T(8,128)(2,1)}, bf16[8,384,128]{2,1,0:T(8,128)(2,1)}, bf16[8,384,128]{2,1,0:T(8,128)(2,1)}) custom-call(f32[8,384]{1,0:T(8,128)} %get-tuple-element.112.upper_ref, f32[8,384]{1,0:T(8,128)} %get-tuple-element.107.lower_ref, f32[8,384]{1,0:T(8,128)} %get-tuple-element.128.mant_ref, ...), custom_call_target="tpu_custom_call" | custom-call | flops 18874368 | bytes 4718592 | tf_op jit(solution)/shard_map/legendre/pallas_call | solution.py:120
  139.3 2.2 fusion.34
  158.6 16.8 %collective-permute-done.2 = bf16[8,2,384,128]{3,2,1,0:T(8,128)(2,1)} collective-permute-done((bf16[8,2,384,128]{3,2,1,0:T(8,128)(2,1)}, bf16[8,2,384,128]{3,2,1,0:T(8,128)(2,1)}, u32[]{:S(2)}, u32[]{:S(2)}) %collective-permute-start.2) | collective-permute-done | bytes 1572896 | tf_op jit(solution)/shard_map/ppermute | solution.py:232
  180.3 6.6 %all-to-all-start.4 = ((bf16[16,1,8,8,2,128]{5,2,4,3,1,0:T(8,128)(2,1)}), bf16[16,1,8,8,2,128]{5,2,4,3,1,0:T(8,128)(2,1)}, u32[]{:S(2)}, u32[]{:S(2)}) async-start(bf16[16,1,8,8,2,128]{5,2,4,3,1,0:T(8,128)(2,1)} %copy.169), calls=%async_computation.4 | async-start | bytes 1048576 | tf_op jit(solution)/shard_map/all_to_all | solution.py:235
  186.9 55.4 %collective-permute-done.4 = bf16[8,2,384,128]{3,2,1,0:T(8,128)(2,1)} collective-permute-done((bf16[8,2,384,128]{3,2,1,0:T(8,128)(2,1)S(1)}, bf16[8,2,384,128]{3,2,1,0:T(8,128)(2,1)}, u32[]{:S(2)}, u32[]{:S(2)}) %collective-permute-start.4) | collective-permute-done | bytes 1572896 | tf_op jit(solution)/shard_map/ppermute | solution.py:232
  242.3 2.4 fusion.24
  247.5 3.8 fusion.28
  251.3 5.8 %all-to-all-start.7 = ((bf16[16,1,8,8,2,128]{5,2,4,3,1,0:T(8,128)(2,1)}), bf16[16,1,8,8,2,128]{5,2,4,3,1,0:T(8,128)(2,1)}, u32[]{:S(2)}, u32[]{:S(2)}) async-start(bf16[16,1,8,8,2,128]{5,2,4,3,1,0:T(8,128)(2,1)} %copy.188), calls=%async_computation.7 | async-start | bytes 1048576 | tf_op jit(solution)/shard_map/all_to_all | solution.py:235
  258.9 3.3 fusion.1
  264.8 6.7 %all-to-all-done.7 = bf16[16,1,8,8,2,128]{5,2,4,3,1,0:T(8,128)(2,1)} async-done(((bf16[16,1,8,8,2,128]{5,2,4,3,1,0:T(8,128)(2,1)}), bf16[16,1,8,8,2,128]{5,2,4,3,1,0:T(8,128)(2,1)}, u32[]{:S(2)}, u32[]{:S(2)}) %all-to-all-start.7) | async-done | bytes 524320 | tf_op jit(solution)/shard_map/all_to_all | solution.py:235
  271.4 4.3 all-to-all-start.6
  275.8 2.3 fusion.40
  284.5 14.2 %all-to-all-done.6 = bf16[16,2,8,8,2,128]{5,2,4,3,1,0:T(8,128)(2,1)} async-done(((bf16[16,2,8,8,2,128]{5,2,4,3,1,0:T(8,128)(2,1)}), bf16[16,2,8,8,2,128]{5,2,4,3,1,0:T(8,128)(2,1)}, u32[]{:S(2)}, u32[]{:S(2)}) %all-to-all-start.6) | async-done | bytes 1048608 | tf_op jit(solution)/shard_map/all_to_all | solution.py:235
  298.7 6.8 %all-to-all-start.5 = ((bf16[16,2,8,8,2,128]{5,2,4,3,1,0:T(8,128)(2,1)}), bf16[16,2,8,8,2,128]{5,2,4,3,1,0:T(8,128)(2,1)}, u32[]{:S(2)}, u32[]{:S(2)}) async-start(bf16[16,2,8,8,2,128]{5,2,4,3,1,0:T(8,128)(2,1)} %copy.254), calls=%async_computation.5 | async-start | bytes 2097152 | tf_op jit(solution)/shard_map/all_to_all | solution.py:235
  308.8 7.8 %dynamic-slice_bitcast_fusion = (bf16[1,24,720,128]{3,2,1,0:T(8,128)(2,1)}, bf16[1,24,720,128]{3,2,1,0:T(8,128)(2,1)}) fusion(bf16[24,128,2,720]{1,3,2,0:T(8,128)(2,1)} %bitcast.334, s32[]{:T(128)S(6)} %select_n.404, s32[]{:T(128)S(6)} %select_n.402), kind=kLoop, calls=%fused_computation.1 | loop fusion | bytes 17694728 | tf_op jit(solution)/shard_map/jit(dynamic_index_in_dim)/dynamic_slice | solution.py:296
  321.2 7.2 %all-to-all-done.5 = bf16[16,2,8,8,2,128]{5,2,4,3,1,0:T(8,128)(2,1)} async-done(((bf16[16,2,8,8,2,128]{5,2,4,3,1,0:T(8,128)(2,1)}), bf16[16,2,8,8,2,128]{5,2,4,3,1,0:T(8,128)(2,1)}, u32[]{:S(2)}, u32[]{:S(2)}) %all-to-all-start.5) | async-done | bytes 1048608 | tf_op jit(solution)/shard_map/all_to_all | solution.py:235
  328.4 7.0 %all-to-all-start.3 = ((bf16[16,3,8,8,2,128]{5,2,4,3,1,0:T(8,128)(2,1)}), bf16[16,3,8,8,2,128]{5,2,4,3,1,0:T(8,128)(2,1)S(1)}, u32[]{:S(2)}, u32[]{:S(2)}) async-start(bf16[16,3,8,8,2,128]{5,2,4,3,1,0:T(8,128)(2,1)} %copy.247), calls=%async_computation.3 | async-start | bytes 3145728 | tf_op jit(solution)/shard_map/all_to_all | solution.py:235
  335.4 6.2 %slice_bitcast_fusion = (bf16[8,720,128]{2,1,0:T(8,128)(2,1)}, bf16[8,720,128]{2,1,0:T(8,128)(2,1)}, bf16[8,720,128]{2,1,0:T(8,128)(2,1)}, bf16[8,720,128]{2,1,0...) fusion(bf16[1,24,720,128]{3,2,1,0:T(8,128)(2,1)} %get-tuple-element.60, ...), kind=kLoop, calls=%fused_computation.52 | loop fusion | bytes 17694720 | tf_op jit(solution)/shard_map/slice | solution.py:299
  355.7 2.3 copy.185
  358.0 2.3 copy.177
  360.4 2.4 fusion.3
  364.4 2.4 fusion.5
  367.3 2.5 fusion.6.refs_4_
  369.8 2.4 fusion.4.refs_4_
  378.6 2.4 fusion.8.refs_4_
  381.0 17.3 %collective-permute-done.8.refs_5_ = bf16[8,720,128]{2,1,0:T(8,128)(2,1)} collective-permute-done((bf16[8,720,128]{2,1,0:T(8,128)(2,1)}, bf16[8,720,128]{2,1,0:T(8,128)(2,1)}, u32[]{:S(2)}, u32[]{:S(2)}) %collective-permute-start.8) | collective-permute-done | bytes 1474592 | tf_op jit(solution)/shard_map/ppermute | solution.py:232
  398.3 9.8 %pointwise.4.refs_6_ = bf16[24,720,256]{2,1,0:T(8,128)(2,1)} custom-call(s32[1]{0:T(128)} %bitcast.refs_0_, f32[720,8]{1,0:T(8,128)} %bitcast.347, bf16[256,512]{1,0:T(8,128)(2,1)} %pad_maximum_fusion.16.refs_2_, bf16[512,256]{1,0:T(8,128)(2,1)} %pad_maximum_fusion.17.refs_3_, bf16[8,720,128]{2,1,0:T(8,128)(2,1)} %fusion.4.refs_4_, ...), custom_call_target="tpu_custom_call" | custom-call | flops 3019898880 | bytes 5898240 | tf_op jit(solution)/shard_map/pointwise/pallas_call | solution.py:201
  408.1 21.8 %collective-permute-done.7.refs_5_ = bf16[8,720,128]{2,1,0:T(8,128)(2,1)} collective-permute-done((bf16[8,720,128]{2,1,0:T(8,128)(2,1)}, bf16[8,720,128]{2,1,0:T(8,128)(2,1)}, u32[]{:S(2)}, u32[]{:S(2)}) %collective-permute-start.7) | collective-permute-done | bytes 1474592 | tf_op jit(solution)/shard_map/ppermute | solution.py:232
  429.9 10.0 %pointwise.5.refs_6_ = bf16[24,720,256]{2,1,0:T(8,128)(2,1)} custom-call(s32[1]{0:T(128)} %bitcast.refs_0_, f32[720,8]{1,0:T(8,128)} %bitcast.348, bf16[256,512]{1,0:T(8,128)(2,1)} %pad_maximum_fusion.16.refs_2_, bf16[512,256]{1,0:T(8,128)(2,1)} %pad_maximum_fusion.17.refs_3_, bf16[8,720,128]{2,1,0:T(8,128)(2,1)} %fusion.6.refs_4_, ...), custom_call_target="tpu_custom_call", output_to_operand_aliasing={{}: (6, {})} | custom-call | flops 3019898880 | bytes 5898240 | tf_op jit(solution)/shard_map/pointwise/pallas_call | solution.py:201
  439.9 5.7 %collective-permute-done.6.refs_5_ = bf16[4,720,128]{2,1,0:T(8,128)(2,1)S(1)} collective-permute-done((bf16[4,720,128]{2,1,0:T(8,128)(2,1)}, bf16[4,720,128]{2,1,0:T(8,128)(2,1)S(1)}, u32[]{:S(2)}, u32[]{:S(2)}) %collective-permute-start.6) | collective-permute-done | bytes 737312 | tf_op jit(solution)/shard_map/ppermute | solution.py:232
  446.5 5.8 %pointwise.6.refs_6_ = bf16[24,720,256]{2,1,0:T(8,128)(2,1)} custom-call(s32[1]{0:T(128)} %bitcast.refs_0_, f32[720,4]{1,0:T(8,128)} %bitcast.346, bf16[256,512]{1,0:T(8,128)(2,1)} %pad_maximum_fusion.16.refs_2_, bf16[512,256]{1,0:T(8,128)(2,1)} %pad_maximum_fusion.17.refs_3_, bf16[8,720,128]{2,1,0:T(8,128)(2,1)} %fusion.8.refs_4_, ...), custom_call_target="tpu_custom_call", output_to_operand_aliasing={{}: (6, {})} | custom-call | flops 1509949440 | bytes 2949120 | tf_op jit(solution)/shard_map/pointwise/pallas_call | solution.py:201
  452.3 8.7 %collective-permute-done.5.refs_5_ = bf16[4,720,128]{2,1,0:T(8,128)(2,1)S(1)} collective-permute-done((bf16[4,720,128]{2,1,0:T(8,128)(2,1)}, bf16[4,720,128]{2,1,0:T(8,128)(2,1)S(1)}, u32[]{:S(2)}, u32[]{:S(2)}) %collective-permute-start.5) | collective-permute-done | bytes 737312 | tf_op jit(solution)/shard_map/ppermute | solution.py:232
  461.8 5.8 %pointwise.7 = bf16[24,720,256]{2,1,0:T(8,128)(2,1)} custom-call(s32[1]{0:T(128)} %bitcast.refs_0_, f32[720,4]{1,0:T(8,128)} %bitcast.345, bf16[256,512]{1,0:T(8,128)(2,1)} %pad_maximum_fusion.16.refs_2_, bf16[512,256]{1,0:T(8,128)(2,1)} %pad_maximum_fusion.17.refs_3_, bf16[8,720,128]{2,1,0:T(8,128)(2,1)} %fusion.8.refs_4_, ...), custom_call_target="tpu_custom_call", output_to_operand_aliasing={{}: (6, {})} | custom-call | flops 1509949440 | bytes 2949120 | tf_op jit(solution)/shard_map/pointwise/pallas_call | solution.py:201
  (232 shorter events, 93.9 us)
Async XLA Ops:
  1.5 9.5 %copy-start.45 = (s32[256]{0:T(256)}, s32[256]{0:T(256)S(1)}, u32[]{:S(2)}) copy-start(s32[256]{0:T(256)S(1)} %mul.691) | copy-start | bytes 3076
  1.7 9.3 %copy-start.43 = (s32[256]{0:T(256)}, s32[256]{0:T(256)S(1)}, u32[]{:S(2)}) copy-start(s32[256]{0:T(256)S(1)} %mul.707) | copy-start | bytes 3076
  2.0 22.3 %copy-start.47 = (s32[256]{0:T(256)}, s32[256]{0:T(256)S(1)}, u32[]{:S(2)}) copy-start(s32[256]{0:T(256)S(1)} %mul.673) | copy-start | bytes 3076
  4.5 19.9 %copy-start.35 = (f32[180,256]{1,0:T(8,128)}, f32[180,256]{1,0:T(8,128)S(1)}, u32[]{:S(2)}) copy-start(f32[180,256]{1,0:T(8,128)S(1)} %get-tuple-element.120) | copy-start | bytes 552964
  4.6 19.9 %copy-start.36 = (f32[180,256]{1,0:T(8,128)}, f32[180,256]{1,0:T(8,128)S(1)}, u32[]{:S(2)}) copy-start(f32[180,256]{1,0:T(8,128)S(1)} %get-tuple-element.121) | copy-start | bytes 552964
  4.6 29.6 %copy-start.33 = (f32[180,256]{1,0:T(8,128)}, f32[180,256]{1,0:T(8,128)S(1)}, u32[]{:S(2)}) copy-start(f32[180,256]{1,0:T(8,128)S(1)} %get-tuple-element.130) | copy-start | bytes 552964
  4.6 29.6 %copy-start.34 = (f32[180,256]{1,0:T(8,128)}, f32[180,256]{1,0:T(8,128)S(1)}, u32[]{:S(2)}) copy-start(f32[180,256]{1,0:T(8,128)S(1)} %get-tuple-element.131) | copy-start | bytes 552964
  13.2 21.0 %slice-start = ((s8[8847360]{0:T(1024)(128)(4,1)}), s8[458752]{0:T(1024)(128)(4,1)S(1)}, s32[]{:S(2)}) async-start(s8[8847360]{0:T(1024)(128)(4,1)} %bitcast.335), calls=%async_computation.8 | async-start | bytes 917504
  13.2 39.5 %all-to-all-start.2 = ((bf16[256,24,128]{2,1,0:T(8,128)(2,1)}), bf16[256,24,128]{2,1,0:T(8,128)(2,1)S(1)}, u32[]{:S(2)}, u32[]{:S(2)}) async-start(bf16[256,24,128]{2,1,0:T(8,128)(2,1)} %copy.155), calls=%async_computation.2 | async-start | bytes 3145728 | tf_op jit(solution)/shard_map/all_to_all | solution.py:235
  20.9 326.8 %collective-permute-start = (bf16[256,256]{1,0:T(8,128)(2,1)}, bf16[256,256]{1,0:T(8,128)(2,1)}, u32[]{:S(2)}, u32[]{:S(2)}) collective-permute-start(bf16[256,256]{1,0:T(8,128)(2,1)} %param.10), channel_id=1, source_target_pairs={{0,1},{1,0},{2,3},{3,2},{4,5},{5,4},{6,7},{7,6},{8,9},{9,8},{10,11... | collective-permute-start | bytes 393224 | tf_op jit(solution)/shard_map/ppermute | solution.py:232
  22.5 326.8 %collective-permute-start.1 = (bf16[256,256]{1,0:T(8,128)(2,1)}, bf16[256,256]{1,0:T(8,128)(2,1)}, u32[]{:S(2)}, u32[]{:S(2)}) collective-permute-start(bf16[256,256]{1,0:T(8,128)(2,1)} %param.11), channel_id=1, source_target_pairs={{0,1},{1,0},{2,3},{3,2},{4,5},{5,4},{6,7},{7,6},{8,9},{9,8},{10,11... | collective-permute-start | bytes 393224 | tf_op jit(solution)/shard_map/ppermute | solution.py:232
  24.4 6.4 %copy-start.40 = (f32[8,256]{1,0:T(8,128)}, f32[8,256]{1,0:T(8,128)S(1)}, u32[]{:S(2)}) copy-start(f32[8,256]{1,0:T(8,128)S(1)} %get-tuple-element.134) | copy-start | bytes 24580
  24.4 6.4 %copy-start.41 = (f32[8,256]{1,0:T(8,128)}, f32[8,256]{1,0:T(8,128)S(1)}, u32[]{:S(2)}) copy-start(f32[8,256]{1,0:T(8,128)S(1)} %get-tuple-element.135) | copy-start | bytes 24580
  24.4 9.8 %slice-start.1 = ((s8[8847360]{0:T(1024)(128)(4,1)}), s8[4194304]{0:T(1024)(128)(4,1)S(1)}, s32[]{:S(2)}) async-start(s8[8847360]{0:T(1024)(128)(4,1)} %bitcast.335), calls=%async_computation.9 | async-start | bytes 8388608
  24.4 9.8 %slice-start.2 = ((s8[8847360]{0:T(1024)(128)(4,1)}), s8[4194304]{0:T(1024)(128)(4,1)S(1)}, s32[]{:S(2)}) async-start(s8[8847360]{0:T(1024)(128)(4,1)} %bitcast.335), calls=%async_computation.10 | async-start | bytes 8388608
  53.9 41.1 %all-to-all-start = ((bf16[256,24,128]{2,1,0:T(8,128)(2,1)}), bf16[256,24,128]{2,1,0:T(8,128)(2,1)}, u32[]{:S(2)}, u32[]{:S(2)}) async-start(bf16[256,24,128]{2,1,0:T(8,128)(2,1)} %copy.143), calls=%async_computation | async-start | bytes 3145728 | tf_op jit(solution)/shard_map/all_to_all | solution.py:235
  66.4 3.7 copy-start.12
  79.3 25.1 %copy-start.42 = (s32[24]{0:T(128)S(1)}, s32[24]{0:T(128)}, u32[]{:S(2)}) copy-start(s32[24]{0:T(128)} %dynamic_slice.54) | copy-start | bytes 292
  79.3 53.1 %copy-start.44 = (s32[256]{0:T(256)S(1)}, s32[256]{0:T(256)}, u32[]{:S(2)}) copy-start(s32[256]{0:T(256)} %copy-done.43) | copy-start | bytes 3076
  79.3 53.6 %copy-start.46 = (s32[256]{0:T(256)S(1)}, s32[256]{0:T(256)}, u32[]{:S(2)}) copy-start(s32[256]{0:T(256)} %copy-done.45) | copy-start | bytes 3076
  79.3 53.6 %copy-start.48 = (s32[256]{0:T(256)S(1)}, s32[256]{0:T(256)}, u32[]{:S(2)}) copy-start(s32[256]{0:T(256)} %copy-done.47) | copy-start | bytes 3076
  94.9 48.1 %all-to-all-start.1 = ((bf16[256,24,128]{2,1,0:T(8,128)(2,1)}), bf16[256,24,128]{2,1,0:T(8,128)(2,1)}, u32[]{:S(2)}, u32[]{:S(2)}) async-start(bf16[256,24,128]{2,1,0:T(8,128)(2,1)} %copy.149), calls=%async_computation.1 | async-start | bytes 3145728 | tf_op jit(solution)/shard_map/all_to_all | solution.py:235
  135.7 3.7 copy-start.11
  137.8 3.7 copy-start.5
  137.8 37.6 %collective-permute-start.2 = (bf16[8,2,384,128]{3,2,1,0:T(8,128)(2,1)}, bf16[8,2,384,128]{3,2,1,0:T(8,128)(2,1)}, u32[]{:S(2)}, u32[]{:S(2)}) collective-permute-start(bf16[8,2,384,128]{3,2,1,0:T(8,128)(2,1)} %bitcast.34), channel_id=1, source_target_pairs={{0,1},{1,0},{2,3},{3,2},{4,5},{5,4},{6,7},{7,6},{8,9},{9,8},{10,11... | collective-permute-start | bytes 4718600 | tf_op jit(solution)/shard_map/ppermute | solution.py:232
  148.7 98.8 %collective-permute-start.3 = (bf16[8,2,384,128]{3,2,1,0:T(8,128)(2,1)}, bf16[8,2,384,128]{3,2,1,0:T(8,128)(2,1)}, u32[]{:S(2)}, u32[]{:S(2)}) collective-permute-start(bf16[8,2,384,128]{3,2,1,0:T(8,128)(2,1)} %bitcast.50), channel_id=1, source_target_pairs={{0,1},{1,0},{2,3},{3,2},{4,5},{5,4},{6,7},{7,6},{8,9},{9,8},{10,11... | collective-permute-start | bytes 4718600 | tf_op jit(solution)/shard_map/ppermute | solution.py:232
  150.2 92.1 %collective-permute-start.4 = (bf16[8,2,384,128]{3,2,1,0:T(8,128)(2,1)S(1)}, bf16[8,2,384,128]{3,2,1,0:T(8,128)(2,1)}, u32[]{:S(2)}, u32[]{:S(2)}) collective-permute-start(bf16[8,2,384,128]{3,2,1,0:T(8,128)(2,1)S(1)} %bitcast.342), channel_id=1, source_target_pairs={{0,1},{1,0},{2,3},{3,2},{4,5},{5,4},{6,7},{7,6},{8,9},{9,8},{10,11... | collective-permute-start | bytes 4718600 | tf_op jit(solution)/shard_map/ppermute | solution.py:232
  156.7 18.7 %copy-start.8 = (bf16[8,2,2,128,128]{4,3,2,0,1:T(8,128)(2,1)S(1)}, bf16[8,2,2,128,128]{4,3,2,0,1:T(8,128)(2,1)}, u32[]{:S(2)}) copy-start(bf16[8,2,2,128,128]{4,3,2,0,1:T(8,128)(2,1)} %pad_maximum_fusion.5) | copy-start | bytes 3145732
  180.3 71.1 %all-to-all-start.4 = ((bf16[16,1,8,8,2,128]{5,2,4,3,1,0:T(8,128)(2,1)}), bf16[16,1,8,8,2,128]{5,2,4,3,1,0:T(8,128)(2,1)}, u32[]{:S(2)}, u32[]{:S(2)}) async-start(bf16[16,1,8,8,2,128]{5,2,4,3,1,0:T(8,128)(2,1)} %copy.169), calls=%async_computation.4 | async-start | bytes 1048576 | tf_op jit(solution)/shard_map/all_to_all | solution.py:235
  186.9 57.9 %copy-start.3 = (f32[8,2,128,384,1]{3,2,1,0,4:T(8,128)S(1)}, f32[8,2,128,384,1]{3,2,1,0,4:T(8,128)}, u32[]{:S(2)}) copy-start(f32[8,2,128,384,1]{3,2,1,0,4:T(8,128)} %copy.294) | copy-start | bytes 9437188
  251.3 20.1 %all-to-all-start.7 = ((bf16[16,1,8,8,2,128]{5,2,4,3,1,0:T(8,128)(2,1)}), bf16[16,1,8,8,2,128]{5,2,4,3,1,0:T(8,128)(2,1)}, u32[]{:S(2)}, u32[]{:S(2)}) async-start(bf16[16,1,8,8,2,128]{5,2,4,3,1,0:T(8,128)(2,1)} %copy.188), calls=%async_computation.7 | async-start | bytes 1048576 | tf_op jit(solution)/shard_map/all_to_all | solution.py:235
  258.9 3.4 copy-start.30
  271.4 27.2 %all-to-all-start.6 = ((bf16[16,2,8,8,2,128]{5,2,4,3,1,0:T(8,128)(2,1)}), bf16[16,2,8,8,2,128]{5,2,4,3,1,0:T(8,128)(2,1)}, u32[]{:S(2)}, u32[]{:S(2)}) async-start(bf16[16,2,8,8,2,128]{5,2,4,3,1,0:T(8,128)(2,1)} %copy.259), calls=%async_computation.6 | async-start | bytes 2097152 | tf_op jit(solution)/shard_map/all_to_all | solution.py:235
  275.8 4.4 copy-start.49
  275.8 5.5 %copy-start.1 = (bf16[8,2,384,128]{2,3,1,0:T(8,128)(2,1)S(1)}, bf16[8,2,384,128]{2,3,1,0:T(8,128)(2,1)}, u32[]{:S(2)}) copy-start(bf16[8,2,384,128]{2,3,1,0:T(8,128)(2,1)} %copy-done) | copy-start | bytes 4718596
  275.8 5.5 %copy-start.28 = (bf16[8,384,128]{2,1,0:T(8,128)(2,1)S(1)}, bf16[8,384,128]{2,1,0:T(8,128)(2,1)}, u32[]{:S(2)}) copy-start(bf16[8,384,128]{2,1,0:T(8,128)(2,1)} %get-tuple-element.49) | copy-start | bytes 2359300
  298.7 29.7 %all-to-all-start.5 = ((bf16[16,2,8,8,2,128]{5,2,4,3,1,0:T(8,128)(2,1)}), bf16[16,2,8,8,2,128]{5,2,4,3,1,0:T(8,128)(2,1)}, u32[]{:S(2)}, u32[]{:S(2)}) async-start(bf16[16,2,8,8,2,128]{5,2,4,3,1,0:T(8,128)(2,1)} %copy.254), calls=%async_computation.5 | async-start | bytes 2097152 | tf_op jit(solution)/shard_map/all_to_all | solution.py:235
  308.7 7.8 %copy-start.25 = (bf16[8,384,128]{2,1,0:T(8,128)(2,1)S(1)}, bf16[8,384,128]{2,1,0:T(8,128)(2,1)}, u32[]{:S(2)}) copy-start(bf16[8,384,128]{2,1,0:T(8,128)(2,1)} %get-tuple-element.33) | copy-start | bytes 2359300
  328.4 43.8 %all-to-all-start.3 = ((bf16[16,3,8,8,2,128]{5,2,4,3,1,0:T(8,128)(2,1)}), bf16[16,3,8,8,2,128]{5,2,4,3,1,0:T(8,128)(2,1)S(1)}, u32[]{:S(2)}, u32[]{:S(2)}) async-start(bf16[16,3,8,8,2,128]{5,2,4,3,1,0:T(8,128)(2,1)} %copy.247), calls=%async_computation.3 | async-start | bytes 3145728 | tf_op jit(solution)/shard_map/all_to_all | solution.py:235
  355.7 4.7 %copy-start.23 = (bf16[720,768]{1,0:T(8,128)(2,1)S(1)}, bf16[720,768]{1,0:T(8,128)(2,1)}, u32[]{:S(2)}) copy-start(bf16[720,768]{1,0:T(8,128)(2,1)} %get-tuple-element.46) | copy-start | bytes 3317764
  360.4 4.0 copy-start.19
  362.8 35.5 %collective-permute-start.8 = (bf16[8,720,128]{2,1,0:T(8,128)(2,1)}, bf16[8,720,128]{2,1,0:T(8,128)(2,1)}, u32[]{:S(2)}, u32[]{:S(2)}) collective-permute-start(bf16[8,720,128]{2,1,0:T(8,128)(2,1)} %fusion.3), channel_id=1, source_target_pairs={{0,1},{1,0},{2,3},{3,2},{4,5},{5,4},{6,7},{7,6},{8,9},{9,8},{10,11... | collective-permute-start | bytes 4423688 | tf_op jit(solution)/shard_map/ppermute | solution.py:232
  364.4 3.0 copy-start.21
  366.8 3.0 copy-start.17
  366.8 63.1 %collective-permute-start.7 = (bf16[8,720,128]{2,1,0:T(8,128)(2,1)}, bf16[8,720,128]{2,1,0:T(8,128)(2,1)}, u32[]{:S(2)}, u32[]{:S(2)}) collective-permute-start(bf16[8,720,128]{2,1,0:T(8,128)(2,1)} %fusion.5), channel_id=1, source_target_pairs={{0,1},{1,0},{2,3},{3,2},{4,5},{5,4},{6,7},{7,6},{8,9},{9,8},{10,11... | collective-permute-start | bytes 4423688 | tf_op jit(solution)/shard_map/ppermute | solution.py:232
  375.3 3.3 copy-start.22
  376.6 69.0 %collective-permute-start.6 = (bf16[4,720,128]{2,1,0:T(8,128)(2,1)}, bf16[4,720,128]{2,1,0:T(8,128)(2,1)S(1)}, u32[]{:S(2)}, u32[]{:S(2)}) collective-permute-start(bf16[4,720,128]{2,1,0:T(8,128)(2,1)} %get-tuple-element.73), channel_id=1, source_target_pairs={{0,1},{1,0},{2,3},{3,2},{4,5},{5,4},{6,7},{7,6},{8,9},{9,8},{10,11... | collective-permute-start | bytes 2211848 | tf_op jit(solution)/shard_map/ppermute | solution.py:232
  378.1 82.9 %collective-permute-start.5 = (bf16[4,720,128]{2,1,0:T(8,128)(2,1)}, bf16[4,720,128]{2,1,0:T(8,128)(2,1)S(1)}, u32[]{:S(2)}, u32[]{:S(2)}) collective-permute-start(bf16[4,720,128]{2,1,0:T(8,128)(2,1)} %get-tuple-element.74), channel_id=1, source_target_pairs={{0,1},{1,0},{2,3},{3,2},{4,5},{5,4},{6,7},{7,6},{8,9},{9,8},{10,11... | collective-permute-start | bytes 2211848 | tf_op jit(solution)/shard_map/ppermute | solution.py:232
  (22 other events, 37.7 us)
